TPU v7x, 32 devices: a whole 2x2x4 slice. The times are simulated.
32 devices in a mesh: dom: 16 (over z, x, core), mem: 2 (over y).
Axes of the slice: x: 2, y: 2, z: 4, core: 2. Of those that a mesh axis runs over, the one named last changes fastest.
Arguments:
- ensemble: bfloat16 [12, 32, 65536], P('mem', None, 'dom'), may hold values from -6 to 6
- observed: float32 [32, 16384], P(None, 'dom'), may hold values from -6 to 6
- tile_weight: bfloat16 [1536, 128, 128], P('dom')
- tile_block: int32 [1536], P('dom'), may hold values from 0 to 31
- tile_target: int32 [1536], P('dom'), may hold values from 0 to 127, as said below
- tile_count: int32 [16], P('dom'), may hold values from 48 to 96, as said below
Outputs:
- crps: float32 [32, 16384], P(None, 'dom')
Inputs may be any that keep to these rules, and one draw needn't show every extreme that they name: `tile_block`: a slot's source block, counted within its partition's cells. `tile_target`: slot k belongs to partition p = k // 96; its target tile is owned by one of the partitions p - 4 to p + 4, where partition o owns the 8 target tiles from o * 8 on. The live slots of partition p are the first tile_count[p] of its list; the rest are padding.
All inputs are finite; a program needn't handle non-finite values.
Results may differ from a plain program's by a relative error of at most 0.0003.
Values sent between devices are 32-bit elements; how exact they have to be, the bound alone decides.
A program may use at most 64 MiB of HBM per device.

v0:
```python
import math

import jax
import jax.numpy as jnp
from jax import lax
from jax.sharding import PartitionSpec as P

REACH = 4


def from_behind(value, axis, steps):
    count = lax.axis_size(axis)
    first, last = (max(0, -steps), min(count, count - steps))
    return lax.ppermute(value, axis, [(source, source + steps) for source in range(first, last)])


def pair_total(left_set, right_set):
    flat_left = left_set.reshape(left_set.shape[0], -1)
    flat_right = right_set.reshape(right_set.shape[0], -1)
    total_columns = flat_left.shape[1]
    block_span = math.gcd(total_columns, 1024)

    def block_pairs(first_column):
        left_cols = lax.dynamic_slice_in_dim(flat_left, first_column, block_span, 1)
        right_cols = lax.dynamic_slice_in_dim(flat_right, first_column, block_span, 1)
        return jnp.sum(jnp.abs(left_cols[:, None, :] - right_cols[None, :, :]), axis=(0, 1))

    column_starts = jnp.arange(total_columns // block_span, dtype=jnp.int32) * block_span
    return lax.map(block_pairs, column_starts).reshape(left_set.shape[1:])


def on_device(ensemble, observed, tile_weight, tile_block, tile_target, tile_count):
    groups, levels, src_cells = ensemble.shape
    block_cells = tile_weight.shape[1]
    channels = groups * levels
    tile_slots = tile_block.shape[0]
    values = ensemble.reshape(channels, src_cells // block_cells, block_cells)
    picked = jnp.take(values, tile_block, axis=1)
    partial_value = jnp.einsum(
        "csi,sij->scj", picked, tile_weight, preferred_element_type=jnp.float32
    )
    owned = observed.shape[1] // block_cells
    window = 2 * REACH + 1
    device = lax.axis_index("dom")
    local_tile = tile_target - (device - REACH) * owned
    rows_index = jnp.arange(window * owned, dtype=jnp.int32)
    is_live = jnp.arange(tile_slots, dtype=jnp.int32) < tile_count[0]
    chooser = ((rows_index[:, None] == local_tile[None, :]) & is_live[None, :]).astype(jnp.float32)
    owner_parts = jnp.dot(
        chooser,
        partial_value.reshape(tile_slots, channels * block_cells),
        precision=lax.Precision.HIGHEST,
        preferred_element_type=jnp.float32,
    )
    owner_parts = owner_parts.reshape(window, owned, channels * block_cells)
    summed = owner_parts[REACH]
    for offset in range(-REACH, REACH + 1):
        if offset != 0:
            summed = summed + from_behind(owner_parts[REACH + offset], "dom", offset)
    remapped = (
        summed.reshape(owned, groups, levels, block_cells)
        .transpose(1, 2, 0, 3)
        .reshape(groups, levels, owned * block_cells)
    )
    members = groups * lax.axis_size("mem")
    norm_pairs = 2.0 * members * (members - 1)
    regrouped = lax.all_to_all(remapped, "mem", split_axis=2, concat_axis=0, tiled=True)
    part_cells = regrouped.shape[2]
    observed_part = lax.dynamic_slice_in_dim(
        observed, lax.axis_index("mem") * part_cells, part_cells, 1
    )
    skill_sum = jnp.sum(jnp.abs(regrouped - observed_part[None]), axis=0)
    spread = pair_total(regrouped, regrouped)
    score_part = skill_sum / members - spread / norm_pairs
    return lax.all_gather(score_part, "mem", axis=1, tiled=True)


def solution(mesh):
    return jax.shard_map(
        on_device,
        mesh=mesh,
        in_specs=(
            P("mem", None, "dom"),
            P(None, "dom"),
            P("dom", None, None),
            P("dom"),
            P("dom"),
            P("dom"),
        ),
        out_specs=P(None, "dom"),
        check_vma=False,
    )
```

profile of v0, /device:TPU:0, one launch (start us, length us, event | category | flops | bytes accessed | tf_op | source)
XLA Modules:
  0.0 214.5 jit_solution(2916523083471834512)
XLA Ops:
  0.0 0.8 compare_select_fusion
  0.8 0.8 compare_and_fusion
  1.6 1.7 copy.18
  3.4 1.8 copy.13
  5.9 4.8 %gather_fusion = bf16[96,192,128]{2,1,0:T(8,128)(2,1)} fusion(bf16[192,32,128]{2,0,1:T(8,128)(2,1)} %copy.13, s32[1024]{0:T(1024)S(1)} %pad_clamp_fusion), kind=kCustom, calls=%fused_computation | custom fusion | bytes 9437568 | tf_op jit(solution)/shard_map/jit(_take)/gather | solution.py:38
  10.7 3.4 %fusion.3 = f32[96,192,128]{2,1,0:T(8,128)S(1)} fusion(bf16[96,128,128]{2,1,0:T(8,128)(2,1)S(1)} %copy-done, bf16[96,192,128]{2,1,0:T(8,128)(2,1)} %gather_fusion, pred[96]{0:T(512)(128)(4,1)S(1)} %compare_and_fusion), kind=kOutput, calls=%fused_computation.6 | convolution fusion | flops 606339072 | bytes 17301600 | tf_op jit(solution)/shard_map/csi,sij->scj/dot_general | solution.py:39
  14.1 10.0 %fusion = f32[72,24576]{1,0:T(8,128)S(1)} fusion(f32[12,8,192,128]{3,2,1,0:T(8,128)S(1)} %bitcast.32, s32[96]{0:T(128)S(1)} %broadcast_subtract_fusion, pred[96]{0:T(512)(128)(4,1)S(1)} %iota_compare_fusion.1), kind=kOutput, calls=%fused_computation.3 | convolution fusion | flops 2038445568 | bytes 16515552 | tf_op jit(solution)/shard_map/dot_general | solution.py:49
  24.5 1.3 collective-permute-start
  25.8 1.3 collective-permute-start.1
  27.1 1.3 collective-permute-start.2
  28.4 1.3 collective-permute-start.3
  29.7 3.1 %collective-permute-start.4 = (f32[8,24576]{1,0:T(8,128)S(1)}, f32[8,24576]{1,0:T(8,128)S(1)}, u32[]{:S(2)}, u32[]{:S(2)}) collective-permute-start(f32[8,24576]{1,0:T(8,128)S(1)} %get-tuple-element.54), channel_id=1, source_target_pairs={{0,2},{2,4},{4,6},{6,8},{8,10},{10,12},{12,14},{14,16},{16,18},{18... | collective-permute-start | bytes 2359304 | tf_op jit(solution)/shard_map/ppermute | solution.py:14
  32.8 15.1 %collective-permute-done = f32[8,24576]{1,0:T(8,128)S(1)} collective-permute-done((f32[8,24576]{1,0:T(8,128)S(1)}, f32[8,24576]{1,0:T(8,128)S(1)}, u32[]{:S(2)}, u32[]{:S(2)}) %collective-permute-start) | collective-permute-done | bytes 786464 | tf_op jit(solution)/shard_map/ppermute | solution.py:14
  47.9 2.7 %collective-permute-start.5 = (f32[8,24576]{1,0:T(8,128)S(1)}, f32[8,24576]{1,0:T(8,128)S(1)}, u32[]{:S(2)}, u32[]{:S(2)}) collective-permute-start(f32[8,24576]{1,0:T(8,128)S(1)} %get-tuple-element.53), channel_id=1, source_target_pairs={{0,4},{2,6},{4,8},{6,10},{8,12},{10,14},{12,16},{14,18},{16,20},{1... | collective-permute-start | bytes 2359304 | tf_op jit(solution)/shard_map/ppermute | solution.py:14
  50.6 8.3 %collective-permute-start.6 = (f32[8,24576]{1,0:T(8,128)S(1)}, f32[8,24576]{1,0:T(8,128)S(1)}, u32[]{:S(2)}, u32[]{:S(2)}) collective-permute-start(f32[8,24576]{1,0:T(8,128)S(1)} %get-tuple-element.52), channel_id=1, source_target_pairs={{0,6},{2,8},{4,10},{6,12},{8,14},{10,16},{12,18},{14,20},{16,22},{... | collective-permute-start | bytes 2359304 | tf_op jit(solution)/shard_map/ppermute | solution.py:14
  59.0 30.4 %collective-permute-start.7 = (f32[8,24576]{1,0:T(8,128)S(1)}, f32[8,24576]{1,0:T(8,128)S(1)}, u32[]{:S(2)}, u32[]{:S(2)}) collective-permute-start(f32[8,24576]{1,0:T(8,128)S(1)} %get-tuple-element.51), channel_id=1, source_target_pairs={{0,8},{2,10},{4,12},{6,14},{8,16},{10,18},{12,20},{14,22},{16,24},... | collective-permute-start | bytes 2359304 | tf_op jit(solution)/shard_map/ppermute | solution.py:14
  89.4 8.5 %collective-permute-done.5 = f32[8,24576]{1,0:T(8,128)S(1)} collective-permute-done((f32[8,24576]{1,0:T(8,128)S(1)}, f32[8,24576]{1,0:T(8,128)S(1)}, u32[]{:S(2)}, u32[]{:S(2)}) %collective-permute-start.5) | collective-permute-done | bytes 786464 | tf_op jit(solution)/shard_map/ppermute | solution.py:14
  98.0 8.4 %collective-permute-done.6 = f32[8,24576]{1,0:T(8,128)S(1)} collective-permute-done((f32[8,24576]{1,0:T(8,128)S(1)}, f32[8,24576]{1,0:T(8,128)S(1)}, u32[]{:S(2)}, u32[]{:S(2)}) %collective-permute-start.6) | collective-permute-done | bytes 786464 | tf_op jit(solution)/shard_map/ppermute | solution.py:14
  106.4 1.2 fusion.14
  107.6 4.3 %copy.14 = f32[6,32,8,128]{1,0,3,2:T(8,128)} copy(f32[6,32,8,128]{3,2,1,0:T(8,128)} %bitcast.39) | data formatting | bytes 1572864 | tf_op jit(solution)/shard_map/transpose | solution.py:62
  111.9 4.0 %reshape.66 = f32[2,1,98304]{2,1,0:T(1,128)} reshape(f32[1024,6,32]{2,1,0:T(8,128)} %bitcast.33) | data formatting | bytes 1572864
  115.9 4.3 %all-to-all-start = ((f32[2,1,98304]{2,1,0:T(1,128)}), f32[2,1,98304]{2,1,0:T(1,128)}, u32[]{:S(2)}, u32[]{:S(2)}) async-start(f32[2,1,98304]{2,1,0:T(1,128)} %reshape.66), calls=%async_computation | async-start | bytes 1572864 | tf_op jit(solution)/shard_map/all_to_all | solution.py:67
  120.3 9.4 %all-to-all-done = f32[2,1,98304]{2,1,0:T(1,128)} async-done(((f32[2,1,98304]{2,1,0:T(1,128)}), f32[2,1,98304]{2,1,0:T(1,128)}, u32[]{:S(2)}, u32[]{:S(2)}) %all-to-all-start) | async-done | bytes 786464 | tf_op jit(solution)/shard_map/all_to_all | solution.py:67
  130.2 5.0 %reduce.1 = f32[2,98304]{1,0:T(2,128)} reduce(f32[2,1,98304]{2,1,0:T(1,128)} %all-to-all-done, f32[]{:T(128)} %broadcast.36), dimensions={1}, to_apply=%all_to_all.11.reduce_sub_computation | reduce | bytes 1572868 | tf_op jit(solution)/shard_map/all_to_all | solution.py:67
  135.2 4.7 %reshape.67 = f32[1024,6,32]{2,1,0:T(8,128)} reshape(f32[2,98304]{1,0:T(2,128)} %reduce.1) | data formatting | bytes 1572864
  140.0 4.4 %copy.17 = f32[6,32,2,512]{3,2,1,0:T(2,128)} copy(f32[6,32,2,512]{1,0,3,2:T(8,128)} %bitcast.34) | data formatting | bytes 1572864 | tf_op jit(solution)/shard_map/all_to_all | solution.py:67
  144.4 1.7 abs_reduce_fusion.1
  146.1 1.3 copy.16
  147.5 1.6 copy.20
  149.1 59.8 %while.11 = (s32[]{:T(128)}, f32[16,1024]{1,0:T(8,128)S(1)}, s32[16]{0:T(128)S(1)}, f32[12,16384]{1,0:T(8,128)}, s32[]{:T(128)}, /*index=5*/s32[]{:T(128)}, s32[]{:T(128)}) while((s32[]{:T(128)}, f32[16,1024]{1,0:T(8,128)S(1)}, s32[16]{0:T(128)S(1)}, f32[12,16384]{1,0:T(8,128)}, s32[]{:T(128)}, /*index=5*/s32[]{:T(128)}, s32[]{:T(128)}) %tuple.31), condition=%wide.region_3.4_spmd, body=%wide.region_1.3_spmd.sunk | while | flops 441349 | bytes 159875 | solution.py:29
  149.1 0.6 dynamic_slice.20
  151.6 1.0 constant_dynamic-slice_fusion.3
  152.8 0.6 dynamic_slice.20
  155.3 1.0 constant_dynamic-slice_fusion.3
  156.6 0.6 dynamic_slice.20
  159.1 1.0 constant_dynamic-slice_fusion.3
  160.3 0.6 dynamic_slice.20
  162.8 1.0 constant_dynamic-slice_fusion.3
  164.0 0.6 dynamic_slice.20
  166.6 1.0 constant_dynamic-slice_fusion.3
  167.8 0.6 dynamic_slice.20
  170.3 1.0 constant_dynamic-slice_fusion.3
  171.5 0.6 dynamic_slice.20
  174.0 1.0 constant_dynamic-slice_fusion.3
  175.3 0.6 dynamic_slice.20
  177.8 1.0 constant_dynamic-slice_fusion.3
  179.0 0.6 dynamic_slice.20
  181.5 1.0 constant_dynamic-slice_fusion.3
  182.7 0.6 dynamic_slice.20
  185.3 1.0 constant_dynamic-slice_fusion.3
  186.5 0.6 dynamic_slice.20
  189.0 1.0 constant_dynamic-slice_fusion.3
  190.2 0.6 dynamic_slice.20
  192.7 1.0 constant_dynamic-slice_fusion.3
  194.0 0.6 dynamic_slice.20
  196.5 1.0 constant_dynamic-slice_fusion.3
  197.7 0.6 dynamic_slice.20
  200.2 1.0 constant_dynamic-slice_fusion.3
  201.4 0.6 dynamic_slice.20
  204.0 1.0 constant_dynamic-slice_fusion.3
  205.2 0.6 dynamic_slice.20
  207.7 0.9 constant_dynamic-slice_fusion.3
  208.9 4.9 %all_gather.3 = f32[32,1024]{1,0:T(8,128)S(1)} all-gather(f32[32,512]{1,0:T(8,128)S(1)} %multiply_subtract_fusion), channel_id=1, replica_groups=mesh['dom'=16,'mem'=2] {'mem'}, dimensions={1}, use_global_device_ids=true | all-gather | bytes 196608 | tf_op jit(solution)/shard_map/all_gather | solution.py:75
  213.9 0.7 copy.34
  (55 shorter events, 4.8 us)
Async XLA Ops:
  0.0 10.7 %copy-start = (bf16[96,128,128]{2,1,0:T(8,128)(2,1)S(1)}, bf16[96,128,128]{2,1,0:T(8,128)(2,1)}, u32[]{:S(2)}) copy-start(bf16[96,128,128]{2,1,0:T(8,128)(2,1)} %param.10) | copy-start | bytes 9437188
  0.0 5.8 %copy-start.2 = (s32[96]{0:T(128)S(1)}, s32[96]{0:T(128)}, u32[]{:S(2)}) copy-start(s32[96]{0:T(128)} %param.12) | copy-start | bytes 1156
  24.5 23.3 %collective-permute-start = (f32[8,24576]{1,0:T(8,128)S(1)}, f32[8,24576]{1,0:T(8,128)S(1)}, u32[]{:S(2)}, u32[]{:S(2)}) collective-permute-start(f32[8,24576]{1,0:T(8,128)S(1)} %get-tuple-element.50), channel_id=1, source_target_pairs={{8,0},{10,2},{12,4},{14,6},{16,8},{18,10},{20,12},{22,14},{24,16},... | collective-permute-start | bytes 2359304 | tf_op jit(solution)/shard_map/ppermute | solution.py:14
  25.8 24.8 %collective-permute-start.1 = (f32[8,24576]{1,0:T(8,128)S(1)}, f32[8,24576]{1,0:T(8,128)S(1)}, u32[]{:S(2)}, u32[]{:S(2)}) collective-permute-start(f32[8,24576]{1,0:T(8,128)S(1)} %get-tuple-element.57), channel_id=1, source_target_pairs={{6,0},{8,2},{10,4},{12,6},{14,8},{16,10},{18,12},{20,14},{22,16},{... | collective-permute-start | bytes 2359304 | tf_op jit(solution)/shard_map/ppermute | solution.py:14
  27.1 31.8 %collective-permute-start.2 = (f32[8,24576]{1,0:T(8,128)S(1)}, f32[8,24576]{1,0:T(8,128)S(1)}, u32[]{:S(2)}, u32[]{:S(2)}) collective-permute-start(f32[8,24576]{1,0:T(8,128)S(1)} %get-tuple-element.56), channel_id=1, source_target_pairs={{4,0},{6,2},{8,4},{10,6},{12,8},{14,10},{16,12},{18,14},{20,16},{2... | collective-permute-start | bytes 2359304 | tf_op jit(solution)/shard_map/ppermute | solution.py:14
  28.4 61.0 %collective-permute-start.3 = (f32[8,24576]{1,0:T(8,128)S(1)}, f32[8,24576]{1,0:T(8,128)S(1)}, u32[]{:S(2)}, u32[]{:S(2)}) collective-permute-start(f32[8,24576]{1,0:T(8,128)S(1)} %get-tuple-element.55), channel_id=1, source_target_pairs={{2,0},{4,2},{6,4},{8,6},{10,8},{12,10},{14,12},{16,14},{18,16},{20... | collective-permute-start | bytes 2359304 | tf_op jit(solution)/shard_map/ppermute | solution.py:14
  29.7 59.7 %collective-permute-start.4 = (f32[8,24576]{1,0:T(8,128)S(1)}, f32[8,24576]{1,0:T(8,128)S(1)}, u32[]{:S(2)}, u32[]{:S(2)}) collective-permute-start(f32[8,24576]{1,0:T(8,128)S(1)} %get-tuple-element.54), channel_id=1, source_target_pairs={{0,2},{2,4},{4,6},{6,8},{8,10},{10,12},{12,14},{14,16},{16,18},{18... | collective-permute-start | bytes 2359304 | tf_op jit(solution)/shard_map/ppermute | solution.py:14
  47.9 50.1 %collective-permute-start.5 = (f32[8,24576]{1,0:T(8,128)S(1)}, f32[8,24576]{1,0:T(8,128)S(1)}, u32[]{:S(2)}, u32[]{:S(2)}) collective-permute-start(f32[8,24576]{1,0:T(8,128)S(1)} %get-tuple-element.53), channel_id=1, source_target_pairs={{0,4},{2,6},{4,8},{6,10},{8,12},{10,14},{12,16},{14,18},{16,20},{1... | collective-permute-start | bytes 2359304 | tf_op jit(solution)/shard_map/ppermute | solution.py:14
  50.6 55.8 %collective-permute-start.6 = (f32[8,24576]{1,0:T(8,128)S(1)}, f32[8,24576]{1,0:T(8,128)S(1)}, u32[]{:S(2)}, u32[]{:S(2)}) collective-permute-start(f32[8,24576]{1,0:T(8,128)S(1)} %get-tuple-element.52), channel_id=1, source_target_pairs={{0,6},{2,8},{4,10},{6,12},{8,14},{10,16},{12,18},{14,20},{16,22},{... | collective-permute-start | bytes 2359304 | tf_op jit(solution)/shard_map/ppermute | solution.py:14
  59.0 47.4 %collective-permute-start.7 = (f32[8,24576]{1,0:T(8,128)S(1)}, f32[8,24576]{1,0:T(8,128)S(1)}, u32[]{:S(2)}, u32[]{:S(2)}) collective-permute-start(f32[8,24576]{1,0:T(8,128)S(1)} %get-tuple-element.51), channel_id=1, source_target_pairs={{0,8},{2,10},{4,12},{6,14},{8,16},{10,18},{12,20},{14,22},{16,24},... | collective-permute-start | bytes 2359304 | tf_op jit(solution)/shard_map/ppermute | solution.py:14
  107.6 12.6 %copy-start.1 = (f32[32,1024]{1,0:T(8,128)S(1)}, f32[32,1024]{1,0:T(8,128)}, u32[]{:S(2)}) copy-start(f32[32,1024]{1,0:T(8,128)} %param.9) | copy-start | bytes 393220
  115.9 13.8 %all-to-all-start = ((f32[2,1,98304]{2,1,0:T(1,128)}), f32[2,1,98304]{2,1,0:T(1,128)}, u32[]{:S(2)}, u32[]{:S(2)}) async-start(f32[2,1,98304]{2,1,0:T(1,128)} %reshape.66), calls=%async_computation | async-start | bytes 1572864 | tf_op jit(solution)/shard_map/all_to_all | solution.py:67
where the time goes:
time: 217 us; the launch traced here: 215 us
  local copies, waits for them, and re-layouts  57.4 us (26%)
  starting transfers between devices  54 us (25%)
  waiting for transfers between devices  41.4 us (19%)
  loops' own time  31 us (14%)
  matrix products  13.4 us (6%)
  other arithmetic  11.4 us (5%)
  blocking collectives  4.93 us (2%)
    ppermute x8, starting transfers between devices, from_behind(): lax.ppermute(value, axis, [(source, source + steps) for source in range(f...  49.7 us
    ppermute x8, waiting for transfers between devices, from_behind(): lax.ppermute(value, axis, [(source, source + steps) for source in range(f...  32 us
    another operation x1, loops' own time, pair_total(): return lax.map(block_pairs, column_starts).reshape(left_set.shape[1:])  31 us
    dynamic_slice x16, local copies, waits for them, and re-layouts, block_pairs(): left_cols = lax.dynamic_slice_in_dim(flat_left, first_column, block_span, 1)  15.5 us
    unnamed x12, local copies, waits for them, and re-layouts  12.9 us
    dot_general x1, matrix products, on_device(): jnp.dot(chooser, partial_value.reshape(tile_slots, channels * block_cells...  10 us
    dynamic_slice x16, local copies, waits for them, and re-layouts, pair_total(): return lax.map(block_pairs, column_starts).reshape(left_set.shape[1:])  9.73 us
    all_to_all x1, waiting for transfers between devices, on_device(): lax.all_to_all(remapped, 'mem', split_axis=2, concat_axis=0, tiled=True)  9.41 us
  transfers between devices with their start and end apart: 9, of which 4 were waited for; matrix products, arithmetic and copies ran while one was open for 0% of the time, Pallas kernels for 0%

commit v1 on v0

v1 whole, which is shorter than its diff:
```python
import functools
import math

import jax
import jax.numpy as jnp
from jax import lax
from jax.experimental import pallas as pl
from jax.experimental.pallas import tpu as pltpu
from jax.sharding import PartitionSpec as P

REACH = 4
PAIR = 2
HALF = REACH // PAIR
UNROLL = 8
MESH = pl.DeviceIdType.MESH


def partial_kernel(unroll, row_ref, block_ref, values_ref, weight_ref, acc_ref):
    step = pl.program_id(0)
    cells = weight_ref.shape[1]

    @pl.when(step == 0)
    def _():
        def clear(row, carry):
            acc_ref[row] = jnp.zeros(acc_ref.shape[1:], jnp.float32)
            return carry

        lax.fori_loop(0, acc_ref.shape[0], clear, 0)

    products = []
    for slot in range(unroll):
        start = pl.multiple_of(block_ref[step * unroll + slot] * cells, cells)
        products.append(
            jnp.dot(
                values_ref[:, pl.ds(start, cells)],
                weight_ref[slot],
                preferred_element_type=jnp.float32,
            )
        )
    for slot in range(unroll):
        acc_ref[row_ref[step * unroll + slot]] += products[slot]


def score_kernel(
    owned, levels, grain, dom_size, mem_size,
    parts_ref, observed_ref, out_ref,
    mine, sib, far, peers, score,
    load_sem, pair_send, pair_recv, far_send, far_recv,
    peer_send, peer_recv, score_send, score_recv,
):
    me = lax.axis_index("dom")
    group = lax.axis_index("mem")
    core = lax.rem(me, PAIR)
    sibling = me + 1 - 2 * core
    share = owned // mem_size
    steps = owned // grain
    share_steps = share // grain
    offsets = [d for k in range(HALF, 0, -1) for d in (k, -k)] + [0]
    chip = lax.div(me, PAIR)
    chips = dom_size // PAIR

    def inside(d):
        return jnp.logical_and(chip + d >= 0, chip + d < chips)

    def tile_at(s):
        return lax.rem((group + 1) * share + s * grain, owned)

    def peer_at(j):
        return lax.rem(group + 1 + j, mem_size)

    def pair_sends(d):
        ok = inside(d)
        if d == HALF:
            ok = jnp.logical_and(ok, core == 1)
        if d == -HALF:
            ok = jnp.logical_and(ok, core == 0)
        return ok

    def pair_gets(d):
        ok = inside(d)
        if d == HALF:
            ok = jnp.logical_and(ok, core == 0)
        if d == -HALF:
            ok = jnp.logical_and(ok, core == 1)
        return ok

    def load(k, d, s):
        row = (PAIR * (d + HALF) + core) * owned + tile_at(s)
        return pltpu.make_async_copy(
            parts_ref.at[pl.ds(row, grain)], mine.at[k, s], load_sem.at[k, s]
        )

    def pair_copy(k, d, s):
        row = (PAIR * (d + HALF) + 1 - core) * owned + tile_at(s)
        return pltpu.make_async_remote_copy(
            src_ref=parts_ref.at[pl.ds(row, grain)],
            dst_ref=sib.at[k, s],
            send_sem=pair_send.at[k, s],
            recv_sem=pair_recv.at[k, s],
            device_id={"dom": sibling},
            device_id_type=MESH,
        )

    def far_copy(k, s, target):
        return pltpu.make_async_remote_copy(
            src_ref=mine.at[k, s],
            dst_ref=far.at[k, s],
            send_sem=far_send.at[k, s],
            recv_sem=far_recv.at[k, s],
            device_id={"dom": target},
            device_id_type=MESH,
        )

    own = len(offsets) - 1

    def peer_copy(s):
        j = lax.div(s, share_steps)
        return pltpu.make_async_remote_copy(
            src_ref=mine.at[own, s],
            dst_ref=peers.at[s],
            send_sem=peer_send.at[s],
            recv_sem=peer_recv.at[s],
            device_id={"mem": peer_at(j)},
            device_id_type=MESH,
        )

    def score_copy(j):
        return pltpu.make_async_remote_copy(
            src_ref=score.at[group],
            dst_ref=score.at[group],
            send_sem=score_send.at[j],
            recv_sem=score_recv.at[j],
            device_id={"mem": peer_at(j)},
            device_id_type=MESH,
        )

    def each_step(body):
        def run(s, carry):
            body(s)
            return carry

        lax.fori_loop(0, steps, run, 0)

    barrier = pltpu.get_barrier_semaphore()
    greeted = jnp.int32(mem_size)
    pl.semaphore_signal(barrier, inc=1, device_id={"dom": sibling}, device_id_type=MESH)
    for j in range(mem_size - 1):
        pl.semaphore_signal(barrier, inc=1, device_id={"mem": peer_at(j)}, device_id_type=MESH)
    for d in offsets[:-1]:
        @pl.when(inside(d))
        def _():
            pl.semaphore_signal(
                barrier, inc=1, device_id={"dom": me + PAIR * d}, device_id_type=MESH
            )

        greeted = greeted + inside(d).astype(jnp.int32)

    @each_step
    def _(s):
        for k, d in enumerate(offsets):
            @pl.when(inside(d))
            def _():
                load(k, d, s).start()

    pl.semaphore_wait(barrier, greeted)

    @each_step
    def _(s):
        for k, d in enumerate(offsets):
            @pl.when(pair_sends(d))
            def _():
                pair_copy(k, d, s).start()

    @each_step
    def _(s):
        for k, d in enumerate(offsets):
            @pl.when(inside(d))
            def _():
                load(k, d, s).wait()

                @pl.when(pair_gets(d))
                def _():
                    pair_copy(k, d, s).wait_recv()
                    mine[k, s] += sib[k, s]

                if d != 0:
                    far_copy(k, s, me + PAIR * d).start()

    @each_step
    def _(s):
        for k, d in enumerate(offsets[:-1]):
            @pl.when(inside(-d))
            def _():
                far_copy(k, s, sibling).wait_recv()
                mine[own, s] += far[k, s]

        if mem_size > 1:
            @pl.when(s < steps - share_steps)
            def _():
                peer_copy(s).start()

    if mem_size > 1:
        def take(s, carry):
            peer_copy(s).wait_recv()
            return carry

        lax.fori_loop(0, steps - share_steps, take, 0)

    groups = mine.shape[3] // levels
    members = groups * mem_size
    rows = 8
    cells = mine.shape[4]
    chunks = levels // rows
    first = steps - share_steps

    def score_chunk(index, carry):
        t = lax.div(index, chunks)
        low = pl.multiple_of(lax.rem(index, chunks) * rows, rows)
        part, place = lax.div(t, grain), lax.rem(t, grain)
        fields = []
        for g in range(groups):
            at = pl.ds(low + g * levels, rows)
            fields.append(mine[own, first + part, place, at, :])
            for j in range(mem_size - 1):
                fields.append(peers[j * share_steps + part, place, at, :])
        seen = observed_ref[
            pl.ds(low, rows), pl.ds(pl.multiple_of((group * share + t) * cells, cells), cells)
        ]
        skill = jnp.abs(fields[0] - seen)
        for field in fields[1:]:
            skill = skill + jnp.abs(field - seen)
        spread = jnp.zeros_like(skill)
        for a in range(members):
            for b in range(a):
                spread = spread + jnp.abs(fields[a] - fields[b])
        score[group, pl.ds(low, rows), pl.ds(pl.multiple_of(t * cells, cells), cells)] = (
            skill / members - spread / (1.0 * members * (members - 1))
        )
        return carry

    lax.fori_loop(0, share * chunks, score_chunk, 0)
    for j in range(mem_size - 1):
        score_copy(j).start()
    for j in range(mem_size - 1):
        score_copy(j).wait_recv()
    for g in range(mem_size):
        out_ref[:, g * share * cells:(g + 1) * share * cells] = score[g]
    for j in range(mem_size - 1):
        score_copy(j).wait_send()

    @each_step
    def _(s):
        for k, d in enumerate(offsets):
            @pl.when(pair_sends(d))
            def _():
                pair_copy(k, d, s).wait_send()

            if d != 0:
                @pl.when(inside(d))
                def _():
                    far_copy(k, s, me + PAIR * d).wait_send()

        if mem_size > 1:
            @pl.when(s < steps - share_steps)
            def _():
                peer_copy(s).wait_send()


def on_device(dom_size, mem_size, ensemble, observed, tile_weight, tile_block, tile_target, tile_count):
    groups, levels, src_cells = ensemble.shape
    cells = tile_weight.shape[1]
    channels = groups * levels
    slots = tile_block.shape[0]
    owned = observed.shape[1] // cells
    window = (2 * REACH + PAIR) * owned
    me = lax.axis_index("dom")
    base = (me - lax.rem(me, PAIR) - REACH) * owned
    is_live = jnp.arange(slots, dtype=jnp.int32) < tile_count[0]
    row = jnp.where(is_live, tile_target - base, window)
    unroll = math.gcd(slots, UNROLL)
    values = ensemble.reshape(channels, src_cells)
    smem = pl.BlockSpec(memory_space=pltpu.SMEM)
    parts = pl.pallas_call(
        functools.partial(partial_kernel, unroll),
        out_shape=jax.ShapeDtypeStruct((window + 1, channels, cells), jnp.float32),
        grid=(slots // unroll,),
        in_specs=[
            smem,
            smem,
            pl.BlockSpec((channels, src_cells), lambda s: (0, 0)),
            pl.BlockSpec((unroll, cells, cells), lambda s: (s, 0, 0)),
        ],
        out_specs=pl.BlockSpec((window + 1, channels, cells), lambda s: (0, 0, 0)),
        compiler_params=pltpu.CompilerParams(vmem_limit_bytes=40 * 2**20),
    )(row, tile_block, values, tile_weight)

    share = owned // mem_size
    grain = math.gcd(share, 2)
    steps = owned // grain
    reach = 2 * HALF + 1
    dma = pltpu.SemaphoreType.DMA
    others = max(mem_size - 1, 1)
    tile = (channels, cells)
    return pl.pallas_call(
        functools.partial(score_kernel, owned, levels, grain, dom_size, mem_size),
        out_shape=jax.ShapeDtypeStruct(observed.shape, jnp.float32),
        in_specs=[
            pl.BlockSpec(memory_space=pl.ANY),
            pl.BlockSpec(memory_space=pltpu.VMEM),
        ],
        out_specs=pl.BlockSpec(memory_space=pltpu.VMEM),
        scratch_shapes=[
            pltpu.VMEM((reach, steps, grain) + tile, jnp.float32),
            pltpu.VMEM((reach, steps, grain) + tile, jnp.float32),
            pltpu.VMEM((reach - 1, steps, grain) + tile, jnp.float32),
            pltpu.VMEM((steps, grain) + tile, jnp.float32),
            pltpu.VMEM((mem_size, levels, share * cells), jnp.float32),
            dma((reach, steps)),
            dma((reach, steps)),
            dma((reach, steps)),
            dma((reach - 1, steps)),
            dma((reach - 1, steps)),
            dma((steps,)),
            dma((steps,)),
            dma((others,)),
            dma((others,)),
        ],
        compiler_params=pltpu.CompilerParams(
            collective_id=0, has_side_effects=True, vmem_limit_bytes=40 * 2**20
        ),
    )(parts, observed)


def solution(mesh):
    return jax.shard_map(
        functools.partial(on_device, mesh.shape["dom"], mesh.shape["mem"]),
        mesh=mesh,
        in_specs=(
            P("mem", None, "dom"),
            P(None, "dom"),
            P("dom", None, None),
            P("dom"),
            P("dom"),
            P("dom"),
        ),
        out_specs=P(None, "dom"),
        check_vma=False,
    )
```

time: 217 us -> 60.3 us (0.28)
  the two profiles are of different devices: /device:TPU:0 before, /device:TPU:16 now
where the time goes in v1:
time: 60.3 us; the launch traced here: 60.1 us
  Pallas kernels  54.2 us (90%)
  local copies, waits for them, and re-layouts  4.61 us (8%)
  between operations  0.68 us (1%)
  other arithmetic  0.66 us (1%)
    pallas_call x1, Pallas kernels, on_device(): pl.pallas_call(functools.partial(score_kernel, owned, levels, grain, dom_...  49.5 us
    pallas_call x1, Pallas kernels, on_device(): pl.pallas_call(functools.partial(partial_kernel, unroll), out_shape=jax.S...  4.66 us
    unnamed x9, local copies, waits for them, and re-layouts  4.61 us

profile of v1, /device:TPU:16, one launch (start us, length us, event | category | flops | bytes accessed | tf_op | source)
XLA Modules:
  0.0 60.1 jit_solution(15207412258810056421)
XLA Ops:
  0.7 0.7 %compare_select_fusion.row_ref = s32[96]{0:T(128)S(1)} fusion(s32[96]{0:T(128)} %param.10, s32[]{:T(128)S(6)} %mul.3, s32[]{:T(128)} %bitcast.2), kind=kLoop, calls=%fused_computation | loop fusion | flops 288 | bytes 776 | tf_op jit(solution)/shard_map/jit(_where)/select_n | solution.py:279
  1.3 0.0 copy-start
  1.3 1.9 %copy-done = bf16[96,128,128]{2,1,0:T(8,128)(2,1)S(1)} copy-done((bf16[96,128,128]{2,1,0:T(8,128)(2,1)S(1)}, bf16[96,128,128]{2,1,0:T(8,128)(2,1)}, u32[]{:S(2)}) %copy-start) | copy-done | bytes 3145752
  3.2 0.0 copy-start.1
  3.2 1.4 %copy-done.1 = bf16[6,32,4096]{2,1,0:T(8,128)(2,1)S(1)} copy-done((bf16[6,32,4096]{2,1,0:T(8,128)(2,1)S(1)}, bf16[6,32,4096]{2,1,0:T(8,128)(2,1)}, u32[]{:S(2)}) %copy-start.1) | copy-done | bytes 1572888
  4.6 0.0 copy-start.3
  4.6 0.7 %copy-done.3 = s32[96]{0:T(128)S(1)} copy-done((s32[96]{0:T(128)S(1)}, s32[96]{0:T(128)}, u32[]{:S(2)}) %copy-start.3) | copy-done | bytes 408
  5.3 0.0 copy-start.2
  5.3 4.7 %shard_map.64.parts_ref = f32[81,192,128]{2,1,0:T(8,128)S(1)} custom-call(s32[96]{0:T(128)S(1)} %compare_select_fusion.row_ref, s32[96]{0:T(128)S(1)} %copy-done.3, bf16[192,4096]{1,0:T(8,128)(2,1)S(1)} %bitcast.3, bf16[96,128,128]{2,1,0:T(8,128)(2,1)S(1)} %copy-done), custom_call_target="tpu_custom_call" | custom-call | tf_op jit(solution)/shard_map/pallas_call | solution.py:283
  9.9 0.0 copy-done.2
  9.9 49.5 %shard_map.65 = f32[32,1024]{1,0:T(8,128)S(1)} custom-call(f32[81,192,128]{2,1,0:T(8,128)S(1)} %shard_map.64.parts_ref, f32[32,1024]{1,0:T(8,128)S(1)} %copy-done.2), custom_call_target="tpu_custom_call" | custom-call | tf_op jit(solution)/shard_map/pallas_call | solution.py:304
  59.5 0.7 %copy.9 = f32[32,1024]{1,0:T(8,128)} copy(f32[32,1024]{1,0:T(8,128)S(1)} %shard_map.65) | data formatting | bytes 262144
Async XLA Ops:
  1.3 1.9 %copy-start = (bf16[96,128,128]{2,1,0:T(8,128)(2,1)S(1)}, bf16[96,128,128]{2,1,0:T(8,128)(2,1)}, u32[]{:S(2)}) copy-start(bf16[96,128,128]{2,1,0:T(8,128)(2,1)} %weight_ref.1) | copy-start | bytes 9437188
  3.2 1.4 %copy-start.1 = (bf16[6,32,4096]{2,1,0:T(8,128)(2,1)S(1)}, bf16[6,32,4096]{2,1,0:T(8,128)(2,1)}, u32[]{:S(2)}) copy-start(bf16[6,32,4096]{2,1,0:T(8,128)(2,1)} %param.6) | copy-start | bytes 4718596
  4.6 0.7 %copy-start.3 = (s32[96]{0:T(128)S(1)}, s32[96]{0:T(128)}, u32[]{:S(2)}) copy-start(s32[96]{0:T(128)} %block_ref.1) | copy-start | bytes 1156
  5.3 4.7 %copy-start.2 = (f32[32,1024]{1,0:T(8,128)S(1)}, f32[32,1024]{1,0:T(8,128)}, u32[]{:S(2)}) copy-start(f32[32,1024]{1,0:T(8,128)} %observed_ref.1) | copy-start | bytes 393220

commit v2 on v0

v2 whole, which is shorter than its diff:
```python
import functools
import math

import jax
import jax.numpy as jnp
from jax import lax
from jax.experimental import pallas as pl
from jax.experimental.pallas import tpu as pltpu
from jax.sharding import PartitionSpec as P

REACH = 4
PAIR = 2
HALF = REACH // PAIR
UNROLL = 8
AHEAD = (1, 2, -1, -2, 0)
MESH = pl.DeviceIdType.MESH


def partial_kernel(
    unroll, owned,
    target_ref, block_ref, count_ref, values_ref, weight_ref, acc_ref,
    targets, blocks, count, values, weights, small_sem, values_sem, weight_sem,
):
    slots, cells = weight_ref.shape[:2]
    window = acc_ref.shape[0] - 1
    me = lax.axis_index("dom")
    base = (me - lax.rem(me, PAIR) - REACH) * owned
    load_values = pltpu.make_async_copy(values_ref, values, values_sem)
    small = [
        pltpu.make_async_copy(block_ref, blocks, small_sem.at[0]),
        pltpu.make_async_copy(target_ref, targets, small_sem.at[1]),
        pltpu.make_async_copy(count_ref, count, small_sem.at[2]),
    ]

    def load_weights(step):
        part = pl.ds(step * unroll, unroll)
        return pltpu.make_async_copy(weight_ref.at[part], weights.at[part], weight_sem.at[step])

    for copy in small:
        copy.start()
    load_values.start()
    for step in range(slots // unroll):
        load_weights(step).start()

    def clear(row, carry):
        acc_ref[row] = jnp.zeros(acc_ref.shape[1:], jnp.float32)
        return carry

    lax.fori_loop(0, window, clear, 0)
    for copy in small:
        copy.wait()
    load_values.wait()

    def add(step, carry):
        load_weights(step).wait()
        products = []
        for k in range(unroll):
            slot = step * unroll + k
            start = pl.multiple_of(blocks[slot] * cells, cells)
            products.append(
                jnp.dot(
                    values[:, pl.ds(start, cells)],
                    weights[slot],
                    preferred_element_type=jnp.float32,
                )
            )
        for k in range(unroll):
            slot = step * unroll + k
            row = jnp.where(slot < count[0], targets[slot] - base, window)
            acc_ref[row] += products[k]
        return carry

    lax.fori_loop(0, slots // unroll, add, 0)


def score_kernel(
    owned, levels, dom_size, mem_size,
    parts_ref, observed_ref, out_ref,
    mine, sib, far, relay, peers, score,
    pair_send, pair_recv, far_send, far_recv, relay_send, relay_recv,
    peer_send, peer_recv, score_send, score_recv,
):
    me = lax.axis_index("dom")
    group = lax.axis_index("mem")
    core = lax.rem(me, PAIR)
    sibling = me + 1 - 2 * core
    share = owned // mem_size
    first = owned - share
    chip = lax.div(me, PAIR)
    chips = dom_size // PAIR
    way = 2 * lax.rem(chip, 2) - 1
    own = len(AHEAD) - 1

    def inside(ahead):
        there = chip + ahead * way
        return jnp.logical_and(there >= 0, there < chips)

    def device_at(ahead):
        return me + PAIR * ahead * way

    def tile_at(s):
        return lax.rem((group + 1) * share + s, owned)

    def peer_at(j):
        return lax.rem(group + 1 + j, mem_size)

    def row_of(k, which, s):
        return (PAIR * (AHEAD[k] * way + HALF) + which) * owned + tile_at(s)

    def reaches(k, which):
        d = AHEAD[k] * way
        over = jnp.logical_and(d == HALF, which == 1)
        under = jnp.logical_and(d == -HALF, which == 0)
        return jnp.logical_and(
            inside(AHEAD[k]), jnp.logical_not(jnp.logical_or(over, under))
        )

    def pair_copy(k, s):
        return pltpu.make_async_remote_copy(
            src_ref=parts_ref.at[row_of(k, 1 - core, s)],
            dst_ref=sib.at[k, s],
            send_sem=pair_send.at[k, s],
            recv_sem=pair_recv.at[k, s],
            device_id={"dom": sibling},
            device_id_type=MESH,
        )

    def far_copy(k, s):
        return pltpu.make_async_remote_copy(
            src_ref=mine.at[k, s],
            dst_ref=far.at[k - 1, s],
            send_sem=far_send.at[k - 1, s],
            recv_sem=far_recv.at[k - 1, s],
            device_id={"dom": device_at(AHEAD[k])},
            device_id_type=MESH,
        )

    def relay_copy(s):
        ahead = 2 - 3 * lax.rem(s, 2)
        return pltpu.make_async_remote_copy(
            src_ref=mine.at[0, s],
            dst_ref=relay.at[s],
            send_sem=relay_send.at[s],
            recv_sem=relay_recv.at[s],
            device_id={"dom": device_at(ahead)},
            device_id_type=MESH,
        )

    def peer_copy(s):
        return pltpu.make_async_remote_copy(
            src_ref=mine.at[own, s],
            dst_ref=peers.at[s],
            send_sem=peer_send.at[s],
            recv_sem=peer_recv.at[s],
            device_id={"mem": peer_at(lax.div(s, share))},
            device_id_type=MESH,
        )

    def score_copy(j, t):
        return pltpu.make_async_remote_copy(
            src_ref=score.at[group, t],
            dst_ref=score.at[group, t],
            send_sem=score_send.at[j, t],
            recv_sem=score_recv.at[j, t],
            device_id={"mem": peer_at(j)},
            device_id_type=MESH,
        )

    def each(start, stop, body):
        def run(s, carry):
            body(s)
            return carry

        lax.fori_loop(start, stop, run, 0)

    def gather_pair(k, s):
        @pl.when(reaches(k, core))
        def _():
            pair_copy(k, s).wait_recv()
            mine[k, s] = parts_ref[row_of(k, core, s)] + sib[k, s]

        @pl.when(jnp.logical_not(reaches(k, core)))
        def _():
            mine[k, s] = parts_ref[row_of(k, core, s)]

    barrier = pltpu.get_barrier_semaphore()
    greeted = jnp.int32(mem_size + 1)
    pl.semaphore_signal(barrier, inc=1, device_id={"dom": sibling}, device_id_type=MESH)
    pl.semaphore_signal(barrier, inc=1, device_id={"dom": device_at(-1)}, device_id_type=MESH)
    for j in range(mem_size - 1):
        pl.semaphore_signal(barrier, inc=1, device_id={"mem": peer_at(j)}, device_id_type=MESH)
    for ahead in (2, -2):
        @pl.when(inside(ahead))
        def _():
            pl.semaphore_signal(
                barrier, inc=1, device_id={"dom": device_at(ahead)}, device_id_type=MESH
            )

        greeted = greeted + inside(ahead).astype(jnp.int32)
    pl.semaphore_wait(barrier, greeted)

    def start_pair(k, s):
        @pl.when(reaches(k, 1 - core))
        def _():
            pair_copy(k, s).start()

    @functools.partial(each, 0, owned)
    def _(s):
        start_pair(0, s)

    @functools.partial(each, 0, owned)
    def _(s):
        for k in range(1, own + 1):
            start_pair(k, s)

    @functools.partial(each, 0, owned)
    def _(s):
        @pl.when(inside(2))
        def _():
            gather_pair(0, s)
            relay_copy(s).start()

    @functools.partial(each, 0, owned)
    def _(s):
        even = lax.rem(s, 2) == 0

        @pl.when(inside(2))
        def _():
            gather_pair(1, s)
            far_copy(1, s).start()

        gather_pair(2, s)

        @pl.when(jnp.logical_not(jnp.logical_and(even, inside(-2))))
        def _():
            far_copy(2, s).start()

        @pl.when(inside(-2))
        def _():
            gather_pair(3, s)

            @pl.when(even)
            def _():
                far_copy(3, s).start()

            relay_copy(s).wait_recv()

            @pl.when(even)
            def _():
                mine[2, s] += relay[s]
                far_copy(2, s).start()

            @pl.when(jnp.logical_not(even))
            def _():
                mine[3, s] += relay[s]
                far_copy(3, s).start()

        gather_pair(own, s)

    def total(s):
        far_copy(2, s).wait_recv()
        mine[own, s] += far[1, s]

        @pl.when(inside(-2))
        def _():
            far_copy(1, s).wait_recv()
            mine[own, s] += far[0, s]

        @pl.when(inside(2))
        def _():
            far_copy(3, s).wait_recv()
            mine[own, s] += far[2, s]

    @functools.partial(each, 0, first)
    def _(s):
        total(s)
        peer_copy(s).start()

    groups = mine.shape[2] // levels
    members = groups * mem_size
    rows = 8
    cells = mine.shape[3]

    @functools.partial(each, 0, share)
    def _(t):
        total(first + t)
        for j in range(mem_size - 1):
            peer_copy(j * share + t).wait_recv()
        column = pl.ds(pl.multiple_of((group * share + t) * cells, cells), cells)

        def score_rows(chunk, carry):
            low = pl.multiple_of(chunk * rows, rows)
            fields = []
            for g in range(groups):
                at = pl.ds(low + g * levels, rows)
                fields.append(mine[own, first + t, at, :])
                for j in range(mem_size - 1):
                    fields.append(peers[j * share + t, at, :])
            seen = observed_ref[pl.ds(low, rows), column]
            skill = jnp.abs(fields[0] - seen)
            for field in fields[1:]:
                skill = skill + jnp.abs(field - seen)
            spread = jnp.zeros_like(skill)
            for a in range(members):
                for b in range(a):
                    spread = spread + jnp.abs(fields[a] - fields[b])
            score[group, t, pl.ds(low, rows), :] = (
                skill / members - spread / (1.0 * members * (members - 1))
            )
            return carry

        lax.fori_loop(0, levels // rows, score_rows, 0)
        for j in range(mem_size - 1):
            score_copy(j, t).start()

    for t in range(share):
        for j in range(mem_size - 1):
            score_copy(j, t).wait_recv()
    for g in range(mem_size):
        for t in range(share):
            at = (g * share + t) * cells
            out_ref[:, at:at + cells] = score[g, t]
    for t in range(share):
        for j in range(mem_size - 1):
            score_copy(j, t).wait_send()

    @functools.partial(each, 0, owned)
    def _(s):
        for k in range(own + 1):
            @pl.when(reaches(k, 1 - core))
            def _():
                pair_copy(k, s).wait_send()

        far_copy(2, s).wait_send()

        @pl.when(inside(2))
        def _():
            relay_copy(s).wait_send()
            far_copy(1, s).wait_send()

        @pl.when(inside(-2))
        def _():
            far_copy(3, s).wait_send()

        @pl.when(s < first)
        def _():
            peer_copy(s).wait_send()


def on_device(dom_size, mem_size, ensemble, observed, tile_weight, tile_block, tile_target, tile_count):
    groups, levels, src_cells = ensemble.shape
    cells = tile_weight.shape[1]
    channels = groups * levels
    slots = tile_block.shape[0]
    owned = observed.shape[1] // cells
    window = (2 * REACH + PAIR) * owned
    unroll = math.gcd(slots, UNROLL)
    values = ensemble.reshape(channels, src_cells)
    dma = pltpu.SemaphoreType.DMA
    hbm = pl.BlockSpec(memory_space=pltpu.HBM)
    vmem = pl.BlockSpec(memory_space=pltpu.VMEM)
    parts = pl.pallas_call(
        functools.partial(partial_kernel, unroll, owned),
        out_shape=jax.ShapeDtypeStruct((window + 1, channels, cells), jnp.float32),
        in_specs=[hbm] * 5,
        out_specs=vmem,
        scratch_shapes=[
            pltpu.SMEM((slots,), jnp.int32),
            pltpu.SMEM((slots,), jnp.int32),
            pltpu.SMEM((1,), jnp.int32),
            pltpu.VMEM(values.shape, values.dtype),
            pltpu.VMEM(tile_weight.shape, tile_weight.dtype),
            dma((3,)),
            dma,
            dma((slots // unroll,)),
        ],
        compiler_params=pltpu.CompilerParams(vmem_limit_bytes=28 * 2**20),
    )(tile_target, tile_block, tile_count, values, tile_weight)

    share = owned // mem_size
    kinds = len(AHEAD)
    others = max(mem_size - 1, 1)
    tile = (channels, cells)
    return pl.pallas_call(
        functools.partial(score_kernel, owned, levels, dom_size, mem_size),
        out_shape=jax.ShapeDtypeStruct(observed.shape, jnp.float32),
        in_specs=[vmem, vmem],
        out_specs=vmem,
        scratch_shapes=[
            pltpu.VMEM((kinds, owned) + tile, jnp.float32),
            pltpu.VMEM((kinds, owned) + tile, jnp.float32),
            pltpu.VMEM((kinds - 2, owned) + tile, jnp.float32),
            pltpu.VMEM((owned,) + tile, jnp.float32),
            pltpu.VMEM((owned,) + tile, jnp.float32),
            pltpu.VMEM((mem_size, share, levels, cells), jnp.float32),
            dma((kinds, owned)),
            dma((kinds, owned)),
            dma((kinds - 2, owned)),
            dma((kinds - 2, owned)),
            dma((owned,)),
            dma((owned,)),
            dma((owned,)),
            dma((owned,)),
            dma((others, share)),
            dma((others, share)),
        ],
        compiler_params=pltpu.CompilerParams(
            collective_id=0, has_side_effects=True, vmem_limit_bytes=36 * 2**20
        ),
    )(parts, observed)


def solution(mesh):
    return jax.shard_map(
        functools.partial(on_device, mesh.shape["dom"], mesh.shape["mem"]),
        mesh=mesh,
        in_specs=(
            P("mem", None, "dom"),
            P(None, "dom"),
            P("dom", None, None),
            P("dom"),
            P("dom"),
            P("dom"),
        ),
        out_specs=P(None, "dom"),
        check_vma=False,
    )
```

time: 217 us -> 47.6 us (0.22); the launches traced: 215 us -> 47.3 us
  starting transfers between devices: 54 us -> 0 us
  local copies, waits for them, and re-layouts: 57.4 us -> 5.26 us
  Pallas kernels: 0 us -> 41.4 us
  waiting for transfers between devices: 41.4 us -> 0 us
  loops' own time: 31 us -> 0 us
  matrix products: 13.4 us -> 0 us
  other arithmetic: 11.4 us -> 0 us
  blocking collectives: 4.93 us -> 0 us
    ppermute x8 -> x0, starting transfers between devices: 49.7 us -> none  [from_behind(): lax.ppermute(value, axis, [(source, source + steps) for source in range(f...]
    pallas_call x0 -> x2, Pallas kernels: none -> 41.4 us  [the longest x1 37 us: on_device(): pl.pallas_call(functools.partial(score_kernel, owned, levels, dom_size, m...]
    ppermute x8 -> x0, waiting for transfers between devices: 32 us -> none  [from_behind(): lax.ppermute(value, axis, [(source, source + steps) for source in range(f...]
    another operation x1 -> x0, loops' own time: 31 us -> none  [pair_total(): return lax.map(block_pairs, column_starts).reshape(left_set.shape[1:])]
    dynamic_slice x33 -> x0, local copies, waits for them, and re-layouts: 25.2 us -> none  [the longest x16 15.5 us: block_pairs(): left_cols = lax.dynamic_slice_in_dim(flat_left, first_column, block_span, 1)]
    dot_general x2 -> x0, matrix products: 13.4 us -> none  [the longest x1 10 us: on_device(): jnp.dot(chooser, partial_value.reshape(tile_slots, channels * block_cells...]
    all_to_all x1 -> x0, waiting for transfers between devices: 9.41 us -> none  [on_device(): lax.all_to_all(remapped, 'mem', split_axis=2, concat_axis=0, tiled=True)]
    unnamed x12 -> x11, local copies, waits for them, and re-layouts: 12.9 us -> 5.26 us
  transfers between devices with their start and end apart: 9 -> 0, of which waited for: 4 -> 0; matrix products, arithmetic and copies ran while one was open for 0% -> 0% of each run, Pallas kernels for 0% -> 0%
where the time goes in v2:
time: 47.6 us; the launch traced here: 47.3 us
  Pallas kernels  41.4 us (87%)
  local copies, waits for them, and re-layouts  5.26 us (11%)
  between operations  0.69 us (1%)
    pallas_call x1, Pallas kernels, on_device(): pl.pallas_call(functools.partial(score_kernel, owned, levels, dom_size, m...  37 us
    unnamed x11, local copies, waits for them, and re-layouts  5.26 us
    pallas_call x1, Pallas kernels, on_device(): pl.pallas_call(functools.partial(partial_kernel, unroll, owned), out_shap...  4.41 us

profile of v2, /device:TPU:0, one launch (start us, length us, event | category | flops | bytes accessed | tf_op | source)
XLA Modules:
  0.0 47.3 jit_solution(1720788323393285491)
XLA Ops:
  0.7 0.0 copy-start
  0.7 1.9 %copy-done = bf16[96,128,128]{2,1,0:T(8,128)(2,1)S(1)} copy-done((bf16[96,128,128]{2,1,0:T(8,128)(2,1)S(1)}, bf16[96,128,128]{2,1,0:T(8,128)(2,1)}, u32[]{:S(2)}) %copy-start) | copy-done | bytes 3145752
  2.5 0.0 copy-start.1
  2.5 1.4 %copy-done.1 = bf16[6,32,4096]{2,1,0:T(8,128)(2,1)S(1)} copy-done((bf16[6,32,4096]{2,1,0:T(8,128)(2,1)S(1)}, bf16[6,32,4096]{2,1,0:T(8,128)(2,1)}, u32[]{:S(2)}) %copy-start.1) | copy-done | bytes 1572888
  4.0 0.0 copy-start.3
  4.0 0.7 %copy-done.3 = s32[96]{0:T(128)S(1)} copy-done((s32[96]{0:T(128)S(1)}, s32[96]{0:T(128)}, u32[]{:S(2)}) %copy-start.3) | copy-done | bytes 408
  4.6 0.0 copy-start.4
  4.6 0.7 %copy-done.4 = s32[96]{0:T(128)S(1)} copy-done((s32[96]{0:T(128)S(1)}, s32[96]{0:T(128)}, u32[]{:S(2)}) %copy-start.4) | copy-done | bytes 408
  5.3 0.0 copy-start.2
  5.3 4.4 %shard_map.64.parts_ref = f32[81,192,128]{2,1,0:T(8,128)S(1)} custom-call(s32[96]{0:T(128)S(1)} %copy-done.3, s32[96]{0:T(128)S(1)} %copy-done.4, s32[1]{0:T(128)S(6)} %copy.8.count_ref, bf16[192,4096]{1,0:T(8,128)(2,1)S(1)} %bitcast.1, bf16[96,128,128]{2,1,0:T(8,128)(2,1)S(1)} %copy-done), custom_call_target="tpu_custom_call" | custom-call | tf_op jit(solution)/shard_map/pallas_call | solution.py:362
  9.7 0.0 copy-done.2
  9.7 37.0 %shard_map.65 = f32[32,1024]{1,0:T(8,128)S(1)} custom-call(f32[81,192,128]{2,1,0:T(8,128)S(1)} %shard_map.64.parts_ref, f32[32,1024]{1,0:T(8,128)S(1)} %copy-done.2), custom_call_target="tpu_custom_call" | custom-call | tf_op jit(solution)/shard_map/pallas_call | solution.py:384
  46.7 0.7 %copy.9 = f32[32,1024]{1,0:T(8,128)} copy(f32[32,1024]{1,0:T(8,128)S(1)} %shard_map.65) | data formatting | bytes 262144
Async XLA Ops:
  0.7 1.9 %copy-start = (bf16[96,128,128]{2,1,0:T(8,128)(2,1)S(1)}, bf16[96,128,128]{2,1,0:T(8,128)(2,1)}, u32[]{:S(2)}) copy-start(bf16[96,128,128]{2,1,0:T(8,128)(2,1)} %weight_ref.1) | copy-start | bytes 9437188
  2.5 1.4 %copy-start.1 = (bf16[6,32,4096]{2,1,0:T(8,128)(2,1)S(1)}, bf16[6,32,4096]{2,1,0:T(8,128)(2,1)}, u32[]{:S(2)}) copy-start(bf16[6,32,4096]{2,1,0:T(8,128)(2,1)} %param.6) | copy-start | bytes 4718596
  4.0 0.7 %copy-start.3 = (s32[96]{0:T(128)S(1)}, s32[96]{0:T(128)}, u32[]{:S(2)}) copy-start(s32[96]{0:T(128)} %target_ref.1) | copy-start | bytes 1156
  4.6 0.7 %copy-start.4 = (s32[96]{0:T(128)S(1)}, s32[96]{0:T(128)}, u32[]{:S(2)}) copy-start(s32[96]{0:T(128)} %block_ref.1) | copy-start | bytes 1156
  5.3 4.4 %copy-start.2 = (f32[32,1024]{1,0:T(8,128)S(1)}, f32[32,1024]{1,0:T(8,128)}, u32[]{:S(2)}) copy-start(f32[32,1024]{1,0:T(8,128)} %observed_ref.1) | copy-start | bytes 393220

commit v3 on v2

--- a/solution.py
+++ b/solution.py
@@ -11,52 +11,28 @@
 REACH = 4
 PAIR = 2
 HALF = REACH // PAIR
-UNROLL = 8
+UNROLL = 32
 AHEAD = (1, 2, -1, -2, 0)
 MESH = pl.DeviceIdType.MESH
 
 
 def partial_kernel(
-    unroll, owned,
-    target_ref, block_ref, count_ref, values_ref, weight_ref, acc_ref,
-    targets, blocks, count, values, weights, small_sem, values_sem, weight_sem,
+    unroll, shift,
+    packed, values, weights, acc_ref,
 ):
-    slots, cells = weight_ref.shape[:2]
+    slots, cells = weights.shape[:2]
     window = acc_ref.shape[0] - 1
-    me = lax.axis_index("dom")
-    base = (me - lax.rem(me, PAIR) - REACH) * owned
-    load_values = pltpu.make_async_copy(values_ref, values, values_sem)
-    small = [
-        pltpu.make_async_copy(block_ref, blocks, small_sem.at[0]),
-        pltpu.make_async_copy(target_ref, targets, small_sem.at[1]),
-        pltpu.make_async_copy(count_ref, count, small_sem.at[2]),
-    ]
-
-    def load_weights(step):
-        part = pl.ds(step * unroll, unroll)
-        return pltpu.make_async_copy(weight_ref.at[part], weights.at[part], weight_sem.at[step])
-
-    for copy in small:
-        copy.start()
-    load_values.start()
-    for step in range(slots // unroll):
-        load_weights(step).start()
 
     def clear(row, carry):
         acc_ref[row] = jnp.zeros(acc_ref.shape[1:], jnp.float32)
         return carry
 
     lax.fori_loop(0, window, clear, 0)
-    for copy in small:
-        copy.wait()
-    load_values.wait()
-
     def add(step, carry):
-        load_weights(step).wait()
         products = []
         for k in range(unroll):
             slot = step * unroll + k
-            start = pl.multiple_of(blocks[slot] * cells, cells)
+            start = pl.multiple_of((packed[slot] & ((1 << shift) - 1)) * cells, cells)
             products.append(
                 jnp.dot(
                     values[:, pl.ds(start, cells)],
@@ -66,8 +42,7 @@
             )
         for k in range(unroll):
             slot = step * unroll + k
-            row = jnp.where(slot < count[0], targets[slot] - base, window)
-            acc_ref[row] += products[k]
+            acc_ref[packed[slot] >> shift] += products[k]
         return carry
 
     lax.fori_loop(0, slots // unroll, add, 0)
@@ -355,27 +330,22 @@
     owned = observed.shape[1] // cells
     window = (2 * REACH + PAIR) * owned
     unroll = math.gcd(slots, UNROLL)
+    me = lax.axis_index("dom")
+    base = (me - lax.rem(me, PAIR) - REACH) * owned
+    is_live = jnp.arange(slots, dtype=jnp.int32) < tile_count[0]
+    shift = (src_cells // cells - 1).bit_length()
+    packed = (jnp.where(is_live, tile_target - base, window) << shift) + tile_block
     values = ensemble.reshape(channels, src_cells)
     dma = pltpu.SemaphoreType.DMA
-    hbm = pl.BlockSpec(memory_space=pltpu.HBM)
+    smem = pl.BlockSpec(memory_space=pltpu.SMEM)
     vmem = pl.BlockSpec(memory_space=pltpu.VMEM)
     parts = pl.pallas_call(
-        functools.partial(partial_kernel, unroll, owned),
+        functools.partial(partial_kernel, unroll, shift),
         out_shape=jax.ShapeDtypeStruct((window + 1, channels, cells), jnp.float32),
-        in_specs=[hbm] * 5,
+        in_specs=[smem] + [vmem] * 2,
         out_specs=vmem,
-        scratch_shapes=[
-            pltpu.SMEM((slots,), jnp.int32),
-            pltpu.SMEM((slots,), jnp.int32),
-            pltpu.SMEM((1,), jnp.int32),
-            pltpu.VMEM(values.shape, values.dtype),
-            pltpu.VMEM(tile_weight.shape, tile_weight.dtype),
-            dma((3,)),
-            dma,
-            dma((slots // unroll,)),
-        ],
         compiler_params=pltpu.CompilerParams(vmem_limit_bytes=28 * 2**20),
-    )(tile_target, tile_block, tile_count, values, tile_weight)
+    )(packed, values, tile_weight)
 
     share = owned // mem_size
     kinds = len(AHEAD)

time: 47.6 us -> 45.9 us (0.964)
  local copies, waits for them, and re-layouts: 5.26 us -> 3.96 us
  Pallas kernels: 41.4 us -> 40.4 us
  other arithmetic: 0 us -> 0.68 us
    unnamed x11 -> x7, local copies, waits for them, and re-layouts: 5.26 us -> 3.96 us
    pallas_call x1, Pallas kernels: 4.41 us -> 3.36 us  [on_device(): pl.pallas_call(functools.partial(partial_kernel, unroll, shift), out_shap...]
    add x0 -> x1, other arithmetic: none -> 0.68 us  [on_device(): (jnp.where(is_live, tile_target - base, window) << shift) + tile_block]
where the time goes in v3:
time: 45.9 us; the launch traced here: 45.7 us
  Pallas kernels  40.4 us (88%)
  local copies, waits for them, and re-layouts  3.96 us (9%)
  other arithmetic  0.68 us (1%)
  between operations  0.68 us (1%)
    pallas_call x1, Pallas kernels, on_device(): pl.pallas_call(functools.partial(score_kernel, owned, levels, dom_size, m...  37 us
    unnamed x7, local copies, waits for them, and re-layouts  3.96 us
    pallas_call x1, Pallas kernels, on_device(): pl.pallas_call(functools.partial(partial_kernel, unroll, shift), out_shap...  3.36 us

profile of v3, /device:TPU:0, one launch (start us, length us, event | category | flops | bytes accessed | tf_op | source)
XLA Modules:
  0.0 45.7 jit_solution(15441184011250906365)
XLA Ops:
  0.7 0.7 %fusion.1.packed = s32[96]{0:T(128)S(1)} fusion(s32[96]{0:T(128)} %param.9, s32[96]{0:T(128)} %param.10, s32[]{:T(128)S(6)} %mul.3, s32[]{:T(128)} %bitcast.2), kind=kLoop, calls=%fused_computation.2 | loop fusion | flops 480 | bytes 1160 | tf_op jit(solution)/shard_map/add | solution.py:337
  1.3 0.0 copy-start
  1.3 1.9 %copy-done = bf16[96,128,128]{2,1,0:T(8,128)(2,1)S(1)} copy-done((bf16[96,128,128]{2,1,0:T(8,128)(2,1)S(1)}, bf16[96,128,128]{2,1,0:T(8,128)(2,1)}, u32[]{:S(2)}) %copy-start) | copy-done | bytes 3145752
  3.2 0.0 copy-start.1
  3.2 1.4 %copy-done.1 = bf16[6,32,4096]{2,1,0:T(8,128)(2,1)S(1)} copy-done((bf16[6,32,4096]{2,1,0:T(8,128)(2,1)S(1)}, bf16[6,32,4096]{2,1,0:T(8,128)(2,1)}, u32[]{:S(2)}) %copy-start.1) | copy-done | bytes 1572888
  4.6 0.0 copy-start.2
  4.6 3.4 %shard_map.64.parts_ref = f32[81,192,128]{2,1,0:T(8,128)S(1)} custom-call(s32[96]{0:T(128)S(1)} %fusion.1.packed, bf16[192,4096]{1,0:T(8,128)(2,1)S(1)} %bitcast.3, bf16[96,128,128]{2,1,0:T(8,128)(2,1)S(1)} %copy-done), custom_call_target="tpu_custom_call" | custom-call | tf_op jit(solution)/shard_map/pallas_call | solution.py:342
  8.0 0.0 copy-done.2
  8.0 37.0 %shard_map.65 = f32[32,1024]{1,0:T(8,128)S(1)} custom-call(f32[81,192,128]{2,1,0:T(8,128)S(1)} %shard_map.64.parts_ref, f32[32,1024]{1,0:T(8,128)S(1)} %copy-done.2), custom_call_target="tpu_custom_call" | custom-call | tf_op jit(solution)/shard_map/pallas_call | solution.py:354
  45.0 0.7 %copy.9 = f32[32,1024]{1,0:T(8,128)} copy(f32[32,1024]{1,0:T(8,128)S(1)} %shard_map.65) | data formatting | bytes 262144
Async XLA Ops:
  1.3 1.9 %copy-start = (bf16[96,128,128]{2,1,0:T(8,128)(2,1)S(1)}, bf16[96,128,128]{2,1,0:T(8,128)(2,1)}, u32[]{:S(2)}) copy-start(bf16[96,128,128]{2,1,0:T(8,128)(2,1)} %weights.1) | copy-start | bytes 9437188
  3.2 1.4 %copy-start.1 = (bf16[6,32,4096]{2,1,0:T(8,128)(2,1)S(1)}, bf16[6,32,4096]{2,1,0:T(8,128)(2,1)}, u32[]{:S(2)}) copy-start(bf16[6,32,4096]{2,1,0:T(8,128)(2,1)} %param.6) | copy-start | bytes 4718596
  4.6 3.4 %copy-start.2 = (f32[32,1024]{1,0:T(8,128)S(1)}, f32[32,1024]{1,0:T(8,128)}, u32[]{:S(2)}) copy-start(f32[32,1024]{1,0:T(8,128)} %observed_ref.1) | copy-start | bytes 393220

commit v4 on v3

--- a/solution.py
+++ b/solution.py
@@ -199,11 +199,6 @@
     def _(s):
         even = lax.rem(s, 2) == 0
 
-        @pl.when(inside(2))
-        def _():
-            gather_pair(1, s)
-            far_copy(1, s).start()
-
         gather_pair(2, s)
 
         @pl.when(jnp.logical_not(jnp.logical_and(even, inside(-2))))
@@ -230,9 +225,13 @@
                 mine[3, s] += relay[s]
                 far_copy(3, s).start()
 
+        @pl.when(inside(2))
+        def _():
+            gather_pair(1, s)
+            far_copy(1, s).start()
+
+    def total(s):
         gather_pair(own, s)
-
-    def total(s):
         far_copy(2, s).wait_recv()
         mine[own, s] += far[1, s]
 

time: 45.9 us -> 45.9 us (level)
  no operation moved by 1% of the time
where the time goes in v4:
time: 45.9 us; the launch traced here: 45.7 us
  Pallas kernels  40.4 us (88%)
  local copies, waits for them, and re-layouts  3.96 us (9%)
  other arithmetic  0.68 us (1%)
  between operations  0.68 us (1%)
    pallas_call x1, Pallas kernels, on_device(): pl.pallas_call(functools.partial(score_kernel, owned, levels, dom_size, m...  37 us
    unnamed x7, local copies, waits for them, and re-layouts  3.96 us
    pallas_call x1, Pallas kernels, on_device(): pl.pallas_call(functools.partial(partial_kernel, unroll, shift), out_shap...  3.38 us

profile of v4, /device:TPU:0, one launch (start us, length us, event | category | flops | bytes accessed | tf_op | source)
XLA Modules:
  0.0 45.7 jit_solution(7155617056338270269)
XLA Ops:
  0.7 0.7 %fusion.1.packed = s32[96]{0:T(128)S(1)} fusion(s32[96]{0:T(128)} %param.9, s32[96]{0:T(128)} %param.10, s32[]{:T(128)S(6)} %mul.3, s32[]{:T(128)} %bitcast.2), kind=kLoop, calls=%fused_computation.2 | loop fusion | flops 480 | bytes 1160 | tf_op jit(solution)/shard_map/add | solution.py:336
  1.3 0.0 copy-start
  1.3 1.9 %copy-done = bf16[96,128,128]{2,1,0:T(8,128)(2,1)S(1)} copy-done((bf16[96,128,128]{2,1,0:T(8,128)(2,1)S(1)}, bf16[96,128,128]{2,1,0:T(8,128)(2,1)}, u32[]{:S(2)}) %copy-start) | copy-done | bytes 3145752
  3.2 0.0 copy-start.1
  3.2 1.4 %copy-done.1 = bf16[6,32,4096]{2,1,0:T(8,128)(2,1)S(1)} copy-done((bf16[6,32,4096]{2,1,0:T(8,128)(2,1)S(1)}, bf16[6,32,4096]{2,1,0:T(8,128)(2,1)}, u32[]{:S(2)}) %copy-start.1) | copy-done | bytes 1572888
  4.6 0.0 copy-start.2
  4.6 3.4 %shard_map.64.parts_ref = f32[81,192,128]{2,1,0:T(8,128)S(1)} custom-call(s32[96]{0:T(128)S(1)} %fusion.1.packed, bf16[192,4096]{1,0:T(8,128)(2,1)S(1)} %bitcast.3, bf16[96,128,128]{2,1,0:T(8,128)(2,1)S(1)} %copy-done), custom_call_target="tpu_custom_call" | custom-call | tf_op jit(solution)/shard_map/pallas_call | solution.py:341
  8.0 0.0 copy-done.2
  8.0 37.0 %shard_map.65 = f32[32,1024]{1,0:T(8,128)S(1)} custom-call(f32[81,192,128]{2,1,0:T(8,128)S(1)} %shard_map.64.parts_ref, f32[32,1024]{1,0:T(8,128)S(1)} %copy-done.2), custom_call_target="tpu_custom_call" | custom-call | tf_op jit(solution)/shard_map/pallas_call | solution.py:353
  45.0 0.7 %copy.9 = f32[32,1024]{1,0:T(8,128)} copy(f32[32,1024]{1,0:T(8,128)S(1)} %shard_map.65) | data formatting | bytes 262144
Async XLA Ops:
  1.3 1.9 %copy-start = (bf16[96,128,128]{2,1,0:T(8,128)(2,1)S(1)}, bf16[96,128,128]{2,1,0:T(8,128)(2,1)}, u32[]{:S(2)}) copy-start(bf16[96,128,128]{2,1,0:T(8,128)(2,1)} %weights.1) | copy-start | bytes 9437188
  3.2 1.4 %copy-start.1 = (bf16[6,32,4096]{2,1,0:T(8,128)(2,1)S(1)}, bf16[6,32,4096]{2,1,0:T(8,128)(2,1)}, u32[]{:S(2)}) copy-start(bf16[6,32,4096]{2,1,0:T(8,128)(2,1)} %param.6) | copy-start | bytes 4718596
  4.6 3.4 %copy-start.2 = (f32[32,1024]{1,0:T(8,128)S(1)}, f32[32,1024]{1,0:T(8,128)}, u32[]{:S(2)}) copy-start(f32[32,1024]{1,0:T(8,128)} %observed_ref.1) | copy-start | bytes 393220
